TPU v7x, 32 devices: a whole 2x2x4 slice. The times are simulated.
32 devices in a mesh: ctx: 8 (over z, x), fsdp: 4 (over y, core).
Axes of the slice: x: 2, y: 2, z: 4, core: 2. Of those that a mesh axis runs over, the one named last changes fastest.
Arguments:
- inputs: bfloat16 [8, 512, 1024], P('fsdp', 'ctx'), may hold values from -6 to 6
- gain_one: bfloat16 [1024], P('fsdp'), may hold values from 0.25 to 1.75
- w_qkv: bfloat16 [1024, 3072], P('fsdp')
- w_attn: bfloat16 [1024, 1024], P('fsdp'), may hold values from -0.75 to 0.75
- gain_two: bfloat16 [1024], P('fsdp'), may hold values from 0.25 to 1.75
- w_in: bfloat16 [1024, 5248], P('fsdp'), may hold values from -0.1875 to 0.1875
- w_ffn: bfloat16 [2624, 1024], P('fsdp'), may hold values from -0.125 to 0.125
- cotangent: bfloat16 [8, 512, 1024], P('fsdp', 'ctx'), may hold values from -6 to 6
Outputs:
- output: bfloat16 [8, 512, 1024], P('fsdp', 'ctx')
- grad_input: float32 [8, 512, 1024], P('fsdp', 'ctx')
- grad_gain_one: float32 [1024], P('fsdp')
- grad_w_qkv: float32 [1024, 3072], P('fsdp')
- grad_w_attn: float32 [1024, 1024], P('fsdp')
- grad_gain_two: float32 [1024], P('fsdp')
- grad_w_in: float32 [1024, 5248], P('fsdp')
- grad_w_ffn: float32 [2624, 1024], P('fsdp')
All inputs are finite; a program needn't handle non-finite values.
Results may differ from a plain program's by a relative error of at most 0.023.
Values may be sent and summed in bfloat16 or wider, within the bound.
A program may use at most 256 MiB of HBM per device.

v0:
```python
import math
import jax
import jax.numpy as jnp
from jax import lax
from jax.sharding import PartitionSpec as P

D = 1024
HEADS = 16
HEAD_DIM = 64
FF = 2624
EPSILON = 1e-05
ROPE_THETA = 160000.0


def norm_parts(values_in):
    mean_val = jnp.mean(values_in, axis=-1, keepdims=True)
    centred = values_in - mean_val
    variance = jnp.mean(centred * centred, axis=-1, keepdims=True)
    inv_std = lax.rsqrt(variance + EPSILON)
    return (centred * inv_std, inv_std)


def norm_back(grad_normed, normed, inv_std):
    return inv_std * (
        grad_normed
        - jnp.mean(grad_normed, axis=-1, keepdims=True)
        - normed * jnp.mean(grad_normed * normed, axis=-1, keepdims=True)
    )


def rotary_tables(positions):
    half_dim = HEAD_DIM // 2
    inv_freq = ROPE_THETA ** (-(jnp.arange(half_dim, dtype=jnp.float32) * 2.0) / HEAD_DIM)
    angles = positions.astype(jnp.float32)[:, None] * inv_freq[None, :]
    cosine = jnp.concatenate([jnp.cos(angles), jnp.cos(angles)], axis=-1)[:, None, :]
    sine_part = jnp.concatenate([jnp.sin(angles), jnp.sin(angles)], axis=-1)[:, None, :]
    return (cosine, sine_part)


def rotate(values_in, cosine, sine_part):
    half_dim = values_in.shape[-1] // 2
    turned = jnp.concatenate([-values_in[..., half_dim:], values_in[..., :half_dim]], axis=-1)
    return values_in * cosine + turned * sine_part


def rotate_back(grads, cosine, sine_part):
    half_dim = grads.shape[-1] // 2
    scaled = grads * sine_part
    turned = jnp.concatenate([scaled[..., half_dim:], -scaled[..., :half_dim]], axis=-1)
    return grads * cosine + turned


def gelu_slope(inner_part):
    cumulative = 0.5 * (1.0 + jax.scipy.special.erf(inner_part * 0.7071067811865476))
    density = jnp.exp(-0.5 * inner_part * inner_part) * 0.3989422804014327
    return cumulative + inner_part * density


def attend_piece(state_in, queries, key_piece, value_piece, scale_factor):
    row_max, row_sum, weighted = state_in
    scores = (
        jnp.einsum("bthd,bshd->bths", queries, key_piece, preferred_element_type=jnp.float32)
        * scale_factor
    )
    new_max = jnp.maximum(row_max, jnp.max(scores, axis=-1))
    rescale = jnp.exp(row_max - new_max)
    exp_vals = jnp.exp(scores - new_max[..., None])
    row_sum = row_sum * rescale + jnp.sum(exp_vals, axis=-1)
    weighted = weighted * rescale[..., None] + jnp.einsum(
        "bths,bshd->bthd",
        exp_vals.astype(jnp.bfloat16),
        value_piece,
        preferred_element_type=jnp.float32,
    )
    return (new_max, row_sum, weighted)


def back_piece(queries, grad_mixed, log_sum, row_delta, key_piece, value_piece, scale_factor):
    scores = (
        jnp.einsum("bthd,bshd->bths", queries, key_piece, preferred_element_type=jnp.float32)
        * scale_factor
    )
    probs = jnp.exp(scores - log_sum[..., None])
    grad_values = jnp.einsum(
        "bths,bthd->bshd",
        probs.astype(jnp.bfloat16),
        grad_mixed,
        preferred_element_type=jnp.float32,
    )
    grad_probs = jnp.einsum(
        "bthd,bshd->bths", grad_mixed, value_piece, preferred_element_type=jnp.float32
    )
    grad_scores = (probs * (grad_probs - row_delta[..., None])).astype(jnp.bfloat16)
    grad_query = (
        jnp.einsum("bths,bshd->bthd", grad_scores, key_piece, preferred_element_type=jnp.float32)
        * scale_factor
    )
    grad_keys = (
        jnp.einsum("bths,bthd->bshd", grad_scores, queries, preferred_element_type=jnp.float32)
        * scale_factor
    )
    return (grad_query, grad_keys, grad_values)


def add_at(whole_grads, piece_grads, offset):
    old_part = lax.dynamic_slice_in_dim(whole_grads, offset, piece_grads.shape[1], 1)
    return lax.dynamic_update_slice_in_dim(whole_grads, old_part + piece_grads, offset, 1)


def on_device(inputs, gain_one, w_qkv, w_attn, gain_two, w_in, w_ffn, cotangent):
    seq_dev = inputs.shape[0]
    tok_seq = inputs.shape[1]
    row_count = seq_dev * tok_seq
    seq_len = tok_seq * lax.axis_size("ctx")
    tokens_f = inputs.reshape(row_count, D).astype(jnp.float32)
    grad_out = cotangent.reshape(row_count, D)
    scale_factor = HEAD_DIM ** (-0.5)
    block_len = math.gcd(seq_len, 512)
    blocks_num = seq_len // block_len
    gathered = (
        lax.all_gather(gain_one, "fsdp", axis=0, tiled=True),
        lax.all_gather(w_qkv, "fsdp", axis=0, tiled=True),
        lax.all_gather(w_attn, "fsdp", axis=0, tiled=True),
        lax.all_gather(gain_two, "fsdp", axis=0, tiled=True),
        lax.all_gather(w_in, "fsdp", axis=0, tiled=True),
        lax.all_gather(w_ffn, "fsdp", axis=0, tiled=True),
    )
    full_g1, full_qkv, full_attn, full_g2, full_in, full_ffn = gathered
    normed_one, inv_one = norm_parts(tokens_f)
    input_one = (normed_one * full_g1.astype(jnp.float32)).astype(jnp.bfloat16)
    project = jnp.dot(input_one, full_qkv, preferred_element_type=jnp.float32)
    positions = lax.axis_index("ctx") * tok_seq + jnp.arange(tok_seq, dtype=jnp.int32)
    cosine, sine_part = rotary_tables(positions)
    shaped = project.reshape(seq_dev, tok_seq, 3, HEADS, HEAD_DIM)
    queries = rotate(shaped[:, :, 0], cosine, sine_part).astype(jnp.bfloat16)
    key_rows = rotate(shaped[:, :, 1], cosine, sine_part).astype(jnp.bfloat16)
    value_rows = shaped[:, :, 2].astype(jnp.bfloat16)
    start_state = (
        jnp.full((seq_dev, tok_seq, HEADS), -jnp.inf, jnp.float32),
        jnp.zeros((seq_dev, tok_seq, HEADS), jnp.float32),
        jnp.zeros((seq_dev, tok_seq, HEADS, HEAD_DIM), jnp.float32),
    )
    whole_keys, whole_values = (
        lax.all_gather(key_rows, "ctx", axis=1, tiled=True),
        lax.all_gather(value_rows, "ctx", axis=1, tiled=True),
    )

    def forward_step(state_in, block_index):
        begin = block_index * block_len
        key_piece = lax.dynamic_slice_in_dim(whole_keys, begin, block_len, 1)
        value_piece = lax.dynamic_slice_in_dim(whole_values, begin, block_len, 1)
        return (attend_piece(state_in, queries, key_piece, value_piece, scale_factor), None)

    state_out, unused = lax.scan(forward_step, start_state, jnp.arange(blocks_num, dtype=jnp.int32))
    row_max, row_sum, weighted = state_out
    attn_f = weighted / row_sum[..., None]
    log_sum = row_max + jnp.log(row_sum)
    attn_b = attn_f.reshape(row_count, D).astype(jnp.bfloat16)
    resid = tokens_f + jnp.dot(attn_b, full_attn, preferred_element_type=jnp.float32)
    normed_two, inv_two = norm_parts(resid)
    input_two = (normed_two * full_g2.astype(jnp.float32)).astype(jnp.bfloat16)
    widened = jnp.dot(input_two, full_in, preferred_element_type=jnp.float32)
    inner_part = widened[:, :FF]
    gating = widened[:, FF:]
    activated = jax.nn.gelu(inner_part, approximate=False)
    hidden = (activated * gating).astype(jnp.bfloat16)
    output = (resid + jnp.dot(hidden, full_ffn, preferred_element_type=jnp.float32)).astype(
        jnp.bfloat16
    )
    back_g1, back_qkv, back_attn, back_g2, back_in, back_ffn = gathered
    grad_ffn = jnp.dot(hidden.T, grad_out, preferred_element_type=jnp.float32)
    grad_hidden = jnp.dot(grad_out, back_ffn.T, preferred_element_type=jnp.float32)
    grad_inner = grad_hidden * gating * gelu_slope(inner_part)
    grad_gating = grad_hidden * activated
    grad_wide = jnp.concatenate([grad_inner, grad_gating], axis=-1).astype(jnp.bfloat16)
    grad_in = jnp.dot(input_two.T, grad_wide, preferred_element_type=jnp.float32)
    grad_normed_two = jnp.dot(grad_wide, back_in.T, preferred_element_type=jnp.float32)
    grad_g2 = jnp.sum(grad_normed_two * normed_two, axis=0)
    grad_resid = grad_out.astype(jnp.float32) + norm_back(
        grad_normed_two * back_g2.astype(jnp.float32), normed_two, inv_two
    )
    part_g2, part_in, part_ffn = (
        lax.psum_scatter(
            grad_g2.astype(jnp.bfloat16), "fsdp", scatter_dimension=0, tiled=True
        ).astype(jnp.float32),
        lax.psum_scatter(
            grad_in.astype(jnp.bfloat16), "fsdp", scatter_dimension=0, tiled=True
        ).astype(jnp.float32),
        lax.psum_scatter(
            grad_ffn.astype(jnp.bfloat16), "fsdp", scatter_dimension=0, tiled=True
        ).astype(jnp.float32),
    )
    resid_b = grad_resid.astype(jnp.bfloat16)
    grad_attn_w = jnp.dot(attn_b.T, resid_b, preferred_element_type=jnp.float32)
    grad_mixed = (
        jnp.dot(resid_b, back_attn.T, preferred_element_type=jnp.float32)
        .astype(jnp.bfloat16)
        .reshape(seq_dev, tok_seq, HEADS, HEAD_DIM)
    )
    row_delta = jnp.sum(grad_mixed.astype(jnp.float32) * attn_f, axis=-1)
    zero_q = jnp.zeros((seq_dev, tok_seq, HEADS, HEAD_DIM), jnp.float32)
    zero_kv = jnp.zeros((seq_dev, seq_len, HEADS, HEAD_DIM), jnp.float32)

    def backward_step(state_in, block_index):
        grad_q_sum, grad_key_all, grad_value_all = state_in
        begin = block_index * block_len
        key_piece = lax.dynamic_slice_in_dim(whole_keys, begin, block_len, 1)
        value_piece = lax.dynamic_slice_in_dim(whole_values, begin, block_len, 1)
        grad_query, grad_keys, grad_values = back_piece(
            queries, grad_mixed, log_sum, row_delta, key_piece, value_piece, scale_factor
        )
        return (
            (
                grad_q_sum + grad_query,
                add_at(grad_key_all, grad_keys, begin),
                add_at(grad_value_all, grad_values, begin),
            ),
            None,
        )

    back_state, unused_back = lax.scan(
        backward_step, (zero_q, zero_kv, zero_kv), jnp.arange(blocks_num, dtype=jnp.int32)
    )
    grad_q_sum, grad_key_all, grad_value_all = back_state
    own_keys, own_values = (
        lax.psum_scatter(
            grad_key_all.astype(jnp.bfloat16), "ctx", scatter_dimension=1, tiled=True
        ).astype(jnp.float32),
        lax.psum_scatter(
            grad_value_all.astype(jnp.bfloat16), "ctx", scatter_dimension=1, tiled=True
        ).astype(jnp.float32),
    )
    grad_q_rot = rotate_back(grad_q_sum, cosine, sine_part).reshape(row_count, D)
    grad_k_rot = rotate_back(own_keys, cosine, sine_part).reshape(row_count, D)
    grad_joint = jnp.concatenate(
        [grad_q_rot, grad_k_rot, own_values.reshape(row_count, D)], axis=-1
    ).astype(jnp.bfloat16)
    grad_qkv = jnp.dot(input_one.T, grad_joint, preferred_element_type=jnp.float32)
    grad_normed_one = jnp.dot(grad_joint, back_qkv.T, preferred_element_type=jnp.float32)
    grad_g1 = jnp.sum(grad_normed_one * normed_one, axis=0)
    grad_input = grad_resid + norm_back(
        grad_normed_one * back_g1.astype(jnp.float32), normed_one, inv_one
    )
    part_g1, part_qkv, part_attn = (
        lax.psum_scatter(
            grad_g1.astype(jnp.bfloat16), "fsdp", scatter_dimension=0, tiled=True
        ).astype(jnp.float32),
        lax.psum_scatter(
            grad_qkv.astype(jnp.bfloat16), "fsdp", scatter_dimension=0, tiled=True
        ).astype(jnp.float32),
        lax.psum_scatter(
            grad_attn_w.astype(jnp.bfloat16), "fsdp", scatter_dimension=0, tiled=True
        ).astype(jnp.float32),
    )
    totals = (
        lax.psum(part_g1.astype(jnp.bfloat16), "ctx").astype(jnp.float32),
        lax.psum(part_qkv.astype(jnp.bfloat16), "ctx").astype(jnp.float32),
        lax.psum(part_attn.astype(jnp.bfloat16), "ctx").astype(jnp.float32),
        lax.psum(part_g2.astype(jnp.bfloat16), "ctx").astype(jnp.float32),
        lax.psum(part_in.astype(jnp.bfloat16), "ctx").astype(jnp.float32),
        lax.psum(part_ffn.astype(jnp.bfloat16), "ctx").astype(jnp.float32),
    )
    return (
        output.reshape(seq_dev, tok_seq, D),
        grad_input.reshape(seq_dev, tok_seq, D),
        totals[0],
        totals[1],
        totals[2],
        totals[3],
        totals[4],
        totals[5],
    )


def solution(mesh):
    return jax.shard_map(
        on_device,
        mesh=mesh,
        in_specs=(
            P("fsdp", "ctx", None),
            P("fsdp"),
            P("fsdp", None),
            P("fsdp", None),
            P("fsdp"),
            P("fsdp", None),
            P("fsdp", None),
            P("fsdp", "ctx", None),
        ),
        out_specs=(
            P("fsdp", "ctx", None),
            P("fsdp", "ctx", None),
            P("fsdp"),
            P("fsdp", None),
            P("fsdp", None),
            P("fsdp"),
            P("fsdp", None),
            P("fsdp", None),
        ),
        check_vma=False,
    )
```

profile of v0, /device:TPU:0, one launch (start us, length us, event | category | flops | bytes accessed | tf_op | source)
XLA Modules:
  0.0 1007.0 jit_solution(11697671415666420469)
XLA Ops:
  8.6 6.0 all-gather.1
  16.9 41.8 %all-gather.10.cloned.1.call-done = bf16[1024,3072]{1,0:T(8,128)(2,1)} async-done(((bf16[256,3072]{1,0:T(8,128)(2,1)}), bf16[1024,3072]{1,0:T(8,128)(2,1)}) %all-gather.10.cloned.1.call-update) | async-done | bytes 6291472 | tf_op jit(solution)/shard_map/all_gather | solution.py:122
  58.7 8.7 copy.36
  89.3 59.0 %all-gather.20.cloned.1.call-done = bf16[2,512,1,16,64]{4,3,2,0,1:T(8,128)(2,1)} async-done(((bf16[2,64,1,16,64]{4,3,2,0,1:T(8,128)(2,1)}), bf16[2,512,1,16,64]{4,3,2,0,1:T(8,128)(2,1)}) %all-gather.20.cloned.1.call-update) | async-done | bytes 2097168 | tf_op jit(solution)/shard_map/all_gather | solution.py:145
  153.7 68.6 %all-gather.12.cloned.1.call-done = bf16[2,512,16,64]{3,2,0,1:T(8,128)(2,1)} async-done(((bf16[2,64,16,64]{3,2,0,1:T(8,128)(2,1)}), bf16[2,512,16,64]{3,2,0,1:T(8,128)(2,1)}) %all-gather.12.cloned.1.call-update) | async-done | bytes 2097168 | tf_op jit(solution)/shard_map/all_gather | solution.py:144
  233.8 11.1 %all-gather.14.cloned.1.call-done = bf16[1024,1024]{1,0:T(8,128)(2,1)} async-done(((bf16[256,1024]{1,0:T(8,128)(2,1)}), bf16[1024,1024]{1,0:T(8,128)(2,1)}) %all-gather.14.cloned.1.call-update) | async-done | bytes 2097168 | tf_op jit(solution)/shard_map/all_gather | solution.py:123
  247.3 70.8 %all-gather.16.cloned.1.call-done = bf16[1024,5248]{1,0:T(8,128)(2,1)} async-done(((bf16[256,5248]{1,0:T(8,128)(2,1)}), bf16[1024,5248]{1,0:T(8,128)(2,1)}) %all-gather.16.cloned.1.call-update) | async-done | bytes 10747920 | tf_op jit(solution)/shard_map/all_gather | solution.py:125
  318.0 7.3 fusion.73
  325.3 35.3 %all-gather.18.cloned.1.call-done = bf16[2624,1024]{1,0:T(8,128)(2,1)} async-done(((bf16[656,1024]{1,0:T(8,128)(2,1)}), bf16[2624,1024]{1,0:T(8,128)(2,1)}) %all-gather.18.cloned.1.call-update) | async-done | bytes 5373968 | tf_op jit(solution)/shard_map/all_gather | solution.py:126
  360.6 8.5 multiply_convert_fusion.1
  386.4 7.4 copy.56
  393.9 6.8 reshape.175
  405.1 7.4 copy.58
  412.5 6.8 reshape.177
  433.2 35.9 %reduce-scatter.19.cloned.1.call-done = bf16[64,2048]{1,0:T(8,128)(2,1)} async-done(((bf16[512,2048]{1,0:T(8,128)(2,1)}), bf16[64,2048]{1,0:T(8,128)(2,1)}) %reduce-scatter.19.cloned.1.call-update) | async-done | bytes 262160
  473.1 67.0 %reduce-scatter.21.cloned.1.call-done = bf16[64,2048]{1,0:T(8,128)(2,1)} async-done(((bf16[512,2048]{1,0:T(8,128)(2,1)}), bf16[64,2048]{1,0:T(8,128)(2,1)}) %reduce-scatter.21.cloned.1.call-update) | async-done | bytes 262160
  553.6 7.0 convolution_convert_fusion
  560.6 12.2 %reduce-scatter.13.cloned.1.call-done = bf16[256,1024]{1,0:T(8,128)(2,1)} async-done(((bf16[1024,1024]{1,0:T(8,128)(2,1)}), bf16[256,1024]{1,0:T(8,128)(2,1)}) %reduce-scatter.13.cloned.1.call-update) | async-done | bytes 524304 | tf_op jit(solution)/shard_map/reduce_scatter | solution.py:251
  572.8 55.2 %reduce-scatter.17.cloned.1.call-done = bf16[656,1024]{1,0:T(8,128)(2,1)} async-done(((bf16[2624,1024]{1,0:T(8,128)(2,1)}), bf16[656,1024]{1,0:T(8,128)(2,1)}) %reduce-scatter.17.cloned.1.call-update) | async-done | bytes 1343504 | tf_op jit(solution)/shard_map/reduce_scatter | solution.py:189
  628.0 61.4 %reduce-scatter.11.cloned.1.call-done = bf16[256,3072]{1,0:T(8,128)(2,1)} async-done(((bf16[1024,3072]{1,0:T(8,128)(2,1)}), bf16[256,3072]{1,0:T(8,128)(2,1)}) %reduce-scatter.11.cloned.1.call-update) | async-done | bytes 1572880 | tf_op jit(solution)/shard_map/reduce_scatter | solution.py:248
  689.4 88.5 %reduce-scatter.15.cloned.1.call-done = bf16[256,5248]{1,0:T(8,128)(2,1)} async-done(((bf16[1024,5248]{1,0:T(8,128)(2,1)}), bf16[256,5248]{1,0:T(8,128)(2,1)}) %reduce-scatter.15.cloned.1.call-update) | async-done | bytes 2686992 | tf_op jit(solution)/shard_map/reduce_scatter | solution.py:186
  784.0 5.7 all-reduce.4
  789.9 22.8 %all-reduce.2 = (bf16[256]{0:T(256)(128)(2,1)S(1)}, bf16[256]{0:T(256)(128)(2,1)S(1)}) all-reduce(bf16[256]{0:T(256)(128)(2,1)S(1)} %dynamic-slice.1, bf16[256]{0:T(256)(128)(2,1)S(1)} %dynamic-slice.3), channel_id=1, replica_groups=mesh['ctx'=8,'fsdp'=4] {'ctx'}, use_global_device_ids=true, to_apply=%region_15.16 | all-reduce | flops 512 | bytes 2048 | tf_op jit(solution)/shard_map/psum | solution.py:256
  814.9 175.5 %all-reduce.7.cloned.1.call-done = (bf16[256,3072]{1,0:T(8,128)(2,1)}, bf16[256,1024]{1,0:T(8,128)(2,1)}, bf16[256,5248]{1,0:T(8,128)(2,1)}, bf16[656,1024]{1,0:T(8,128)(2,1)}) async-done(((bf16[256,3072]{1,0:T(8,128)(2,1)}, bf16[256,1024]{1,0:T(8,128)(2,1)}, bf16[256,5248]{1,0:T(8,128)(2,1)}, bf16[656,1024]{1,0:T(8,128)(2,1)}), (bf16[256,3072]{1,0:T(8,128)(2,1)}, bf16[256,1024]{1,0:T(8,128)(2,1)}, ...) | async-done | bytes 6127632 | tf_op jit(solution)/shard_map/psum | solution.py:257
  (158 shorter events, 115.1 us)
Async XLA Ops:
  7.2 51.5 %all-gather.10.cloned.1.call-start = ((), (), s32[]{:S(2)}) async-start(), calls=%async_computation.6 | async-start | bytes 7864320 | tf_op jit(solution)/shard_map/all_gather | solution.py:122
  7.9 140.4 %all-gather.20.cloned.1.call-start = ((), (), s32[]{:S(2)}) async-start(), calls=%async_computation.15 | async-start | bytes 4718592 | tf_op jit(solution)/shard_map/all_gather | solution.py:145
  58.7 8.7 copy-start.10
  75.4 146.9 %all-gather.12.cloned.1.call-start = ((), (), s32[]{:S(2)}) async-start(), calls=%async_computation.7 | async-start | bytes 4718592 | tf_op jit(solution)/shard_map/all_gather | solution.py:144
  80.4 146.5 %copy-start.12 = (bf16[2,64,16,64]{1,3,2,0:T(8,128)(2,1)}, bf16[2,64,16,64]{1,3,2,0:T(8,128)(2,1)S(1)}, u32[]{:S(2)}) copy-start(bf16[2,64,16,64]{1,3,2,0:T(8,128)(2,1)S(1)} %get-tuple-element.76) | copy-start | bytes 786436
  81.9 163.0 %all-gather.14.cloned.1.call-start = ((), (), s32[]{:S(2)}) async-start(), calls=%async_computation.8 | async-start | bytes 2621440 | tf_op jit(solution)/shard_map/all_gather | solution.py:123
  82.5 235.5 %all-gather.16.cloned.1.call-start = ((), (), s32[]{:S(2)}) async-start(), calls=%async_computation.9 | async-start | bytes 13434880 | tf_op jit(solution)/shard_map/all_gather | solution.py:125
  83.1 277.5 %all-gather.18.cloned.1.call-start = ((), (), s32[]{:S(2)}) async-start(), calls=%async_computation.10 | async-start | bytes 6717440 | tf_op jit(solution)/shard_map/all_gather | solution.py:126
  83.7 385.4 %reduce-scatter.19.cloned.1.call-start = ((), (), s32[]{:S(2)}) async-start(), calls=%async_computation.16 | async-start | bytes 2359296
  227.7 3.2 copy-start.3
  318.0 42.6 %copy-start.17 = (bf16[2,64,1024]{2,1,0:T(8,128)(2,1)S(1)}, bf16[2,64,1024]{2,1,0:T(8,128)(2,1)}, u32[]{:S(2)}) copy-start(bf16[2,64,1024]{2,1,0:T(8,128)(2,1)} %param.15) | copy-start | bytes 786436
  360.6 8.5 copy-start.2
  369.1 3.7 copy-start.19
  369.1 3.7 copy-start.21
  369.1 4.8 copy-start.4
  378.8 5.6 copy-start.13
  400.6 139.4 %reduce-scatter.21.cloned.1.call-start = ((), (), s32[]{:S(2)}) async-start(), calls=%async_computation.17 | async-start | bytes 2359296
  419.3 153.5 %reduce-scatter.13.cloned.1.call-start = ((), (), s32[]{:S(2)}) async-start(), calls=%async_computation.12 | async-start | bytes 2621440 | tf_op jit(solution)/shard_map/reduce_scatter | solution.py:251
  422.5 205.5 %reduce-scatter.17.cloned.1.call-start = ((), (), s32[]{:S(2)}) async-start(), calls=%async_computation.14 | async-start | bytes 6717440 | tf_op jit(solution)/shard_map/reduce_scatter | solution.py:189
  428.8 260.6 %reduce-scatter.11.cloned.1.call-start = ((), (), s32[]{:S(2)}) async-start(), calls=%async_computation.11 | async-start | bytes 7864320 | tf_op jit(solution)/shard_map/reduce_scatter | solution.py:248
  472.0 70.9 %copy-start.11 = (bf16[2,64,1024]{2,1,0:T(8,128)(2,1)S(1)}, bf16[2,64,1024]{2,1,0:T(8,128)(2,1)}, u32[]{:S(2)}) copy-start(bf16[2,64,1024]{2,1,0:T(8,128)(2,1)} %param.8) | copy-start | bytes 786436
  552.5 225.5 %reduce-scatter.15.cloned.1.call-start = ((), (), s32[]{:S(2)}) async-start(), calls=%async_computation.13 | async-start | bytes 13434880 | tf_op jit(solution)/shard_map/reduce_scatter | solution.py:186
  560.6 429.8 %all-reduce.7.cloned.1.call-start = ((), (), s32[]{:S(2)}) async-start(), calls=%async_computation.18 | async-start | bytes 12255232 | tf_op jit(solution)/shard_map/psum | solution.py:257
  779.8 34.0 %copy-start.7 = (f32[128,1024]{1,0:T(8,128)S(1)}, f32[128,1024]{1,0:T(8,128)}, u32[]{:S(2)}) copy-start(f32[128,1024]{1,0:T(8,128)} %copy-done.5) | copy-start | bytes 1572868
  (14 other events, 22.0 us)
Sparse Core Ops, SparseCore 0:
  9.5 49.1 all-gather.9
  75.5 72.7 all-gather.19
  151.0 71.3 all-gather.11
  223.8 21.0 all-gather.13
  246.3 71.6 all-gather.15
  319.4 41.1 all-gather.17
  400.8 68.2 reduce-scatter.18
  472.6 67.3 reduce-scatter.20
  542.6 30.1 reduce-scatter.12
  575.8 52.1 reduce-scatter.16
  630.5 58.8 reduce-scatter.10
  691.9 85.9 reduce-scatter.14
  782.6 207.7 all-reduce.6
where the time goes:
time: 1010 us
  waiting for transfers between devices  785 us (78%)
  local copies, waits for them, and re-layouts  75.1 us (7%)
  matrix products  69.9 us (7%)
  blocking collectives  40.1 us (4%)
  other arithmetic  20.9 us (2%)
  between operations  15.3 us (2%)
    psum x1, waiting for transfers between devices, on_device(): lax.psum(part_qkv.astype(jnp.bfloat16), 'ctx').astype(jnp.float32)  176 us
    unnamed x15, waiting for transfers between devices  105 us
    reduce_scatter x1, waiting for transfers between devices, on_device(): lax.psum_scatter(grad_in.astype(jnp.bfloat16), 'fsdp', scatter_dimension=...  88.5 us
    all_gather x1, waiting for transfers between devices, on_device(): lax.all_gather(w_in, 'fsdp', axis=0, tiled=True)  70.8 us
    all_gather x1, waiting for transfers between devices, on_device(): lax.all_gather(key_rows, 'ctx', axis=1, tiled=True)  68.6 us
    reduce_scatter x1, waiting for transfers between devices, on_device(): lax.psum_scatter(grad_qkv.astype(jnp.bfloat16), 'fsdp', scatter_dimension...  61.4 us
    all_gather x1, waiting for transfers between devices, on_device(): lax.all_gather(value_rows, 'ctx', axis=1, tiled=True)  59 us
    reduce_scatter x1, waiting for transfers between devices, on_device(): lax.psum_scatter(grad_ffn.astype(jnp.bfloat16), 'fsdp', scatter_dimension...  55.2 us
  transfers between devices with their start and end apart: 13, of which 13 were waited for; matrix products, arithmetic and copies ran while one was open for 9% of the time, Pallas kernels for 0%

commit v1 on v0

--- a/solution.py
+++ b/solution.py
@@ -10,6 +10,18 @@
 FF = 2624
 EPSILON = 1e-05
 ROPE_THETA = 160000.0
+
+
+def gather_by_bits(shard, axis, dim):
+    ways, here = (lax.axis_size(axis), lax.axis_index(axis))
+    grown, reach = (shard, 1)
+    while reach < ways:
+        theirs = lax.ppermute(grown, axis, [(d, d ^ reach) for d in range(ways)])
+        mine_first = jnp.concatenate([grown, theirs], axis=dim)
+        theirs_first = jnp.concatenate([theirs, grown], axis=dim)
+        grown = jnp.where(here & reach == 0, mine_first, theirs_first)
+        reach = 2 * reach
+    return grown
 
 
 def norm_parts(values_in):
@@ -142,7 +154,7 @@
     )
     whole_keys, whole_values = (
         lax.all_gather(key_rows, "ctx", axis=1, tiled=True),
-        lax.all_gather(value_rows, "ctx", axis=1, tiled=True),
+        gather_by_bits(value_rows, "ctx", 1),
     )
 
     def forward_step(state_in, block_index):

time: 1010 us -> 989 us (0.979)
  waiting for transfers between devices: 785 us -> 760 us
  local copies, waits for them, and re-layouts: 75.1 us -> 64 us
    all_gather x1 -> x0, waiting for transfers between devices: 59 us -> none  [on_device(): lax.all_gather(value_rows, 'ctx', axis=1, tiled=True)]
    ppermute x0 -> x3, waiting for transfers between devices: none -> 36.2 us  [gather_by_bits(): theirs = lax.ppermute(grown, axis, [(d, d ^ reach) for d in range(ways)])]
    unnamed x64 -> x68, local copies, waits for them, and re-layouts: 45.5 us -> 39.9 us
    unnamed x15 -> x14, waiting for transfers between devices: 105 us -> 106 us
  transfers between devices with their start and end apart: 13 -> 15, of which waited for: 13 -> 14; matrix products, arithmetic and copies ran while one was open for 9% -> 9% of each run, Pallas kernels for 0% -> 0%
where the time goes in v1:
time: 989 us; the launch traced here: 984 us
  waiting for transfers between devices  760 us (77%)
  matrix products  75.2 us (8%)
  local copies, waits for them, and re-layouts  64 us (6%)
  blocking collectives  40.1 us (4%)
  other arithmetic  22.3 us (2%)
  between operations  15.6 us (2%)
    psum x1, waiting for transfers between devices, on_device(): lax.psum(part_qkv.astype(jnp.bfloat16), 'ctx').astype(jnp.float32)  175 us
    unnamed x14, waiting for transfers between devices  106 us
    reduce_scatter x1, waiting for transfers between devices, on_device(): lax.psum_scatter(grad_in.astype(jnp.bfloat16), 'fsdp', scatter_dimension=...  88.6 us
    all_gather x1, waiting for transfers between devices, on_device(): lax.all_gather(w_in, 'fsdp', axis=0, tiled=True)  70.8 us
    all_gather x1, waiting for transfers between devices, on_device(): lax.all_gather(key_rows, 'ctx', axis=1, tiled=True)  66.2 us
    reduce_scatter x1, waiting for transfers between devices, on_device(): lax.psum_scatter(grad_qkv.astype(jnp.bfloat16), 'fsdp', scatter_dimension...  61.3 us
    reduce_scatter x1, waiting for transfers between devices, on_device(): lax.psum_scatter(grad_ffn.astype(jnp.bfloat16), 'fsdp', scatter_dimension...  55.4 us
    all_gather x1, waiting for transfers between devices, on_device(): lax.all_gather(w_qkv, 'fsdp', axis=0, tiled=True)  42.5 us
  transfers between devices with their start and end apart: 15, of which 14 were waited for; matrix products, arithmetic and copies ran while one was open for 9% of the time, Pallas kernels for 0%

profile of v1, /device:TPU:0, one launch (start us, length us, event | category | flops | bytes accessed | tf_op | source)
XLA Modules:
  0.0 983.8 jit_solution(11337642966304465326)
XLA Ops:
  8.6 6.0 all-gather
  16.2 42.5 %all-gather.8.cloned.1.call-done = bf16[1024,3072]{1,0:T(8,128)(2,1)} async-done(((bf16[256,3072]{1,0:T(8,128)(2,1)}), bf16[1024,3072]{1,0:T(8,128)(2,1)}) %all-gather.8.cloned.1.call-update) | async-done | bytes 6291472 | tf_op jit(solution)/shard_map/all_gather | solution.py:134
  58.7 8.6 copy.36
  80.6 18.2 %collective-permute-done = bf16[2,64,16,64]{1,3,2,0:T(8,128)(2,1)S(1)} collective-permute-done((bf16[2,64,16,64]{1,3,2,0:T(8,128)(2,1)S(1)}, bf16[2,64,16,64]{1,3,2,0:T(8,128)(2,1)S(1)}, u32[]{:S(2)}, u32[]{:S(2)}) %collective-permute-start) | collective-permute-done | bytes 262176 | tf_op jit(solution)/shard_map/ppermute | solution.py:19
  100.9 17.9 %collective-permute-done.1 = bf16[2,128,16,64]{1,3,2,0:T(8,128)(2,1)S(1)} collective-permute-done((bf16[2,128,16,64]{1,3,2,0:T(8,128)(2,1)S(1)}, bf16[2,128,16,64]{1,3,2,0:T(8,128)(2,1)S(1)}, u32[]{:S(2)}, u32[]{:S(2)}) %collective-permute-start.1) | collective-permute-done | bytes 524320 | tf_op jit(solution)/shard_map/ppermute | solution.py:19
  128.3 66.2 %all-gather.10.cloned.1.call-done = bf16[2,512,16,64]{3,2,0,1:T(8,128)(2,1)} async-done(((bf16[2,64,16,64]{3,2,0,1:T(8,128)(2,1)}), bf16[2,512,16,64]{3,2,0,1:T(8,128)(2,1)}) %all-gather.10.cloned.1.call-update) | async-done | bytes 2097168 | tf_op jit(solution)/shard_map/all_gather | solution.py:156
  207.6 10.0 %all-gather.12.cloned.1.call-done = bf16[1024,1024]{1,0:T(8,128)(2,1)} async-done(((bf16[256,1024]{1,0:T(8,128)(2,1)}), bf16[1024,1024]{1,0:T(8,128)(2,1)}) %all-gather.12.cloned.1.call-update) | async-done | bytes 2097168 | tf_op jit(solution)/shard_map/all_gather | solution.py:135
  219.9 70.8 %all-gather.14.cloned.1.call-done = bf16[1024,5248]{1,0:T(8,128)(2,1)} async-done(((bf16[256,5248]{1,0:T(8,128)(2,1)}), bf16[1024,5248]{1,0:T(8,128)(2,1)}) %all-gather.14.cloned.1.call-update) | async-done | bytes 10747920 | tf_op jit(solution)/shard_map/all_gather | solution.py:137
  290.7 7.3 fusion.68
  297.9 35.3 %all-gather.16.cloned.1.call-done = bf16[2624,1024]{1,0:T(8,128)(2,1)} async-done(((bf16[656,1024]{1,0:T(8,128)(2,1)}), bf16[2624,1024]{1,0:T(8,128)(2,1)}) %all-gather.16.cloned.1.call-update) | async-done | bytes 5373968 | tf_op jit(solution)/shard_map/all_gather | solution.py:138
  333.3 8.5 multiply_convert_fusion.1
  362.6 7.4 copy.54
  370.0 6.8 reshape.174
  381.4 7.4 copy.56
  388.8 6.8 reshape.176
  408.7 36.6 %reduce-scatter.19.cloned.1.call-done = bf16[64,2048]{1,0:T(8,128)(2,1)} async-done(((bf16[512,2048]{1,0:T(8,128)(2,1)}), bf16[64,2048]{1,0:T(8,128)(2,1)}) %reduce-scatter.19.cloned.1.call-update) | async-done | bytes 262160
  449.3 67.2 %reduce-scatter.21.cloned.1.call-done = bf16[64,2048]{1,0:T(8,128)(2,1)} async-done(((bf16[512,2048]{1,0:T(8,128)(2,1)}), bf16[64,2048]{1,0:T(8,128)(2,1)}) %reduce-scatter.21.cloned.1.call-update) | async-done | bytes 262160
  530.0 7.0 convolution_convert_fusion
  537.1 12.2 %reduce-scatter.13.cloned.1.call-done = bf16[256,1024]{1,0:T(8,128)(2,1)} async-done(((bf16[1024,1024]{1,0:T(8,128)(2,1)}), bf16[256,1024]{1,0:T(8,128)(2,1)}) %reduce-scatter.13.cloned.1.call-update) | async-done | bytes 524304 | tf_op jit(solution)/shard_map/reduce_scatter | solution.py:263
  549.3 55.4 %reduce-scatter.17.cloned.1.call-done = bf16[656,1024]{1,0:T(8,128)(2,1)} async-done(((bf16[2624,1024]{1,0:T(8,128)(2,1)}), bf16[656,1024]{1,0:T(8,128)(2,1)}) %reduce-scatter.17.cloned.1.call-update) | async-done | bytes 1343504 | tf_op jit(solution)/shard_map/reduce_scatter | solution.py:201
  604.7 61.3 %reduce-scatter.11.cloned.1.call-done = bf16[256,3072]{1,0:T(8,128)(2,1)} async-done(((bf16[1024,3072]{1,0:T(8,128)(2,1)}), bf16[256,3072]{1,0:T(8,128)(2,1)}) %reduce-scatter.11.cloned.1.call-update) | async-done | bytes 1572880 | tf_op jit(solution)/shard_map/reduce_scatter | solution.py:260
  665.9 88.6 %reduce-scatter.15.cloned.1.call-done = bf16[256,5248]{1,0:T(8,128)(2,1)} async-done(((bf16[1024,5248]{1,0:T(8,128)(2,1)}), bf16[256,5248]{1,0:T(8,128)(2,1)}) %reduce-scatter.15.cloned.1.call-update) | async-done | bytes 2686992 | tf_op jit(solution)/shard_map/reduce_scatter | solution.py:198
  766.6 22.7 %all-reduce.2 = (bf16[256]{0:T(256)(128)(2,1)S(1)}, bf16[256]{0:T(256)(128)(2,1)S(1)}) all-reduce(bf16[256]{0:T(256)(128)(2,1)S(1)} %dynamic-slice.1, bf16[256]{0:T(256)(128)(2,1)S(1)} %dynamic-slice.3), channel_id=1, replica_groups=mesh['ctx'=8,'fsdp'=4] {'ctx'}, use_global_device_ids=true, to_apply=%region_15.16 | all-reduce | flops 512 | bytes 2048 | tf_op jit(solution)/shard_map/psum | solution.py:268
  791.5 175.4 %all-reduce.7.cloned.1.call-done = (bf16[256,3072]{1,0:T(8,128)(2,1)}, bf16[256,1024]{1,0:T(8,128)(2,1)}, bf16[256,5248]{1,0:T(8,128)(2,1)}, bf16[656,1024]{1,0:T(8,128)(2,1)}) async-done(((bf16[256,3072]{1,0:T(8,128)(2,1)}, bf16[256,1024]{1,0:T(8,128)(2,1)}, bf16[256,5248]{1,0:T(8,128)(2,1)}, bf16[656,1024]{1,0:T(8,128)(2,1)}), (bf16[256,3072]{1,0:T(8,128)(2,1)}, bf16[256,1024]{1,0:T(8,128)(2,1)}, ...) | async-done | bytes 6127632 | tf_op jit(solution)/shard_map/psum | solution.py:269
  (165 shorter events, 122.1 us)
Async XLA Ops:
  7.2 8.8 copy-start.7
  7.2 51.5 %all-gather.8.cloned.1.call-start = ((), (), s32[]{:S(2)}) async-start(), calls=%async_computation.6 | async-start | bytes 7864320 | tf_op jit(solution)/shard_map/all_gather | solution.py:134
  7.9 186.7 %all-gather.10.cloned.1.call-start = ((), (), s32[]{:S(2)}) async-start(), calls=%async_computation.7 | async-start | bytes 4718592 | tf_op jit(solution)/shard_map/all_gather | solution.py:156
  15.9 51.4 %copy-start.20 = (f32[2,64]{1,0:T(2,128)}, f32[2,64]{1,0:T(2,128)S(1)}, u32[]{:S(2)}) copy-start(f32[2,64]{1,0:T(2,128)S(1)} %broadcast_multiply_fusion.3) | copy-start | bytes 1540
  16.2 51.1 %copy-start.23 = (f32[2,64]{1,0:T(2,128)}, f32[2,64]{1,0:T(2,128)S(1)}, u32[]{:S(2)}) copy-start(f32[2,64]{1,0:T(2,128)S(1)} %add_rsqrt_fusion) | copy-start | bytes 1540
  74.2 124.8 %copy-start.9 = (bf16[2,64,16,64]{1,3,2,0:T(8,128)(2,1)}, bf16[2,64,16,64]{1,3,2,0:T(8,128)(2,1)S(1)}, u32[]{:S(2)}) copy-start(bf16[2,64,16,64]{1,3,2,0:T(8,128)(2,1)S(1)} %get-tuple-element.76) | copy-start | bytes 786436
  75.8 141.8 %all-gather.12.cloned.1.call-start = ((), (), s32[]{:S(2)}) async-start(), calls=%async_computation.8 | async-start | bytes 2621440 | tf_op jit(solution)/shard_map/all_gather | solution.py:135
  76.5 214.2 %all-gather.14.cloned.1.call-start = ((), (), s32[]{:S(2)}) async-start(), calls=%async_computation.9 | async-start | bytes 13434880 | tf_op jit(solution)/shard_map/all_gather | solution.py:137
  77.1 256.2 %all-gather.16.cloned.1.call-start = ((), (), s32[]{:S(2)}) async-start(), calls=%async_computation.10 | async-start | bytes 6717440 | tf_op jit(solution)/shard_map/all_gather | solution.py:138
  77.7 367.6 %reduce-scatter.19.cloned.1.call-start = ((), (), s32[]{:S(2)}) async-start(), calls=%async_computation.15 | async-start | bytes 2359296
  79.0 43.7 %copy-start.25 = (bf16[256]{0:T(256)(128)(2,1)S(1)}, bf16[256]{0:T(256)(128)(2,1)}, u32[]{:S(2)}) copy-start(bf16[256]{0:T(256)(128)(2,1)} %param.12) | copy-start | bytes 1540
  79.0 19.8 %collective-permute-start = (bf16[2,64,16,64]{1,3,2,0:T(8,128)(2,1)S(1)}, bf16[2,64,16,64]{1,3,2,0:T(8,128)(2,1)S(1)}, u32[]{:S(2)}, u32[]{:S(2)}) collective-permute-start(bf16[2,64,16,64]{1,3,2,0:T(8,128)(2,1)S(1)} %fusion.51), channel_id=1, source_target_pairs={{0,4},{4,0},{8,12},{12,8},{16,20},{20,16},{24,28},{28,24},{1,5},{5... | collective-permute-start | bytes 786440 | tf_op jit(solution)/shard_map/ppermute | solution.py:19
  99.4 19.5 %collective-permute-start.1 = (bf16[2,128,16,64]{1,3,2,0:T(8,128)(2,1)S(1)}, bf16[2,128,16,64]{1,3,2,0:T(8,128)(2,1)S(1)}, u32[]{:S(2)}, u32[]{:S(2)}) collective-permute-start(bf16[2,128,16,64]{1,3,2,0:T(8,128)(2,1)S(1)} %maximum_select_fusion.2), channel_id=1, source_target_pairs={{0,8},{4,12},{8,0},{12,4},{16,24},{20,28},{24,16},{28,20},{1,9},{5... | collective-permute-start | bytes 1572872 | tf_op jit(solution)/shard_map/ppermute | solution.py:19
  120.3 81.5 %collective-permute-start.2 = (bf16[2,256,16,64]{1,3,2,0:T(8,128)(2,1)}, bf16[2,256,16,64]{1,3,2,0:T(8,128)(2,1)}, u32[]{:S(2)}, u32[]{:S(2)}) collective-permute-start(bf16[2,256,16,64]{1,3,2,0:T(8,128)(2,1)} %maximum_select_fusion.1), channel_id=1, source_target_pairs={{0,16},{4,20},{8,24},{12,28},{16,0},{20,4},{24,8},{28,12},{1,17},{... | collective-permute-start | bytes 3145736 | tf_op jit(solution)/shard_map/ppermute | solution.py:19
  290.7 42.6 %copy-start.14 = (bf16[2,64,1024]{2,1,0:T(8,128)(2,1)S(1)}, bf16[2,64,1024]{2,1,0:T(8,128)(2,1)}, u32[]{:S(2)}) copy-start(bf16[2,64,1024]{2,1,0:T(8,128)(2,1)} %param.15) | copy-start | bytes 786436
  346.3 49.6 %copy-start.4 = (f32[128,1024]{1,0:T(8,128)}, f32[128,1024]{1,0:T(8,128)S(1)}, u32[]{:S(2)}) copy-start(f32[128,1024]{1,0:T(8,128)S(1)} %multiply_add_fusion.1) | copy-start | bytes 1572868
  376.8 139.7 %reduce-scatter.21.cloned.1.call-start = ((), (), s32[]{:S(2)}) async-start(), calls=%async_computation.16 | async-start | bytes 2359296
  395.6 153.7 %reduce-scatter.13.cloned.1.call-start = ((), (), s32[]{:S(2)}) async-start(), calls=%async_computation.12 | async-start | bytes 2621440 | tf_op jit(solution)/shard_map/reduce_scatter | solution.py:263
  398.0 206.7 %reduce-scatter.17.cloned.1.call-start = ((), (), s32[]{:S(2)}) async-start(), calls=%async_computation.14 | async-start | bytes 6717440 | tf_op jit(solution)/shard_map/reduce_scatter | solution.py:201
  404.4 261.5 %reduce-scatter.11.cloned.1.call-start = ((), (), s32[]{:S(2)}) async-start(), calls=%async_computation.11 | async-start | bytes 7864320 | tf_op jit(solution)/shard_map/reduce_scatter | solution.py:260
  448.2 71.2 %copy-start.8 = (bf16[2,64,1024]{2,1,0:T(8,128)(2,1)S(1)}, bf16[2,64,1024]{2,1,0:T(8,128)(2,1)}, u32[]{:S(2)}) copy-start(bf16[2,64,1024]{2,1,0:T(8,128)(2,1)} %param.8) | copy-start | bytes 786436
  529.0 225.6 %reduce-scatter.15.cloned.1.call-start = ((), (), s32[]{:S(2)}) async-start(), calls=%async_computation.13 | async-start | bytes 13434880 | tf_op jit(solution)/shard_map/reduce_scatter | solution.py:198
  537.1 429.9 %all-reduce.7.cloned.1.call-start = ((), (), s32[]{:S(2)}) async-start(), calls=%async_computation.17 | async-start | bytes 12255232 | tf_op jit(solution)/shard_map/psum | solution.py:269
  756.5 34.0 %copy-start.5 = (f32[128,1024]{1,0:T(8,128)S(1)}, f32[128,1024]{1,0:T(8,128)}, u32[]{:S(2)}) copy-start(f32[128,1024]{1,0:T(8,128)} %copy-done.4) | copy-start | bytes 1572868
  (18 other events, 54.3 us)
Sparse Core Ops, SparseCore 0:
  9.5 49.0 all-gather.7
  75.9 118.6 all-gather.9
  196.1 21.3 all-gather.11
  219.0 71.6 all-gather.13
  292.1 41.1 all-gather.15
  376.9 68.2 reduce-scatter.18
  448.8 67.6 reduce-scatter.20
  519.0 30.2 reduce-scatter.12
  552.5 52.1 reduce-scatter.16
  607.1 58.8 reduce-scatter.10
  668.6 85.9 reduce-scatter.14
  759.2 207.7 all-reduce.6
